TPU v7x, 128 devices: a whole 4x4x4 slice. The times are simulated.
128 devices in a mesh: bx: 16 (over x, z), by: 8 (over y, core).
Axes of the slice: x: 4, y: 4, z: 4, core: 2. Of those that a mesh axis runs over, the one named last changes fastest.
Arguments:
- features: bfloat16 [16, 8, 1024, 128], P('bx', 'by'), may hold values from -13 to 13
- live_count: int32 [16, 8], P('bx', 'by'), may hold values from 128 to 1024, as said below
- neighbour_map: int32 [16, 8, 27, 1024], P('bx', 'by'), may hold values from 0 to 2175, as said below
- send_rows: int32 [16, 8, 8, 128], P('bx', 'by'), may hold values from 0 to 1023, as said below
- weight: bfloat16 [3456, 128], replicated, may hold values from -0.109375 to 0.109375
- gain: float32 [128], replicated, may hold values from 0.5 to 1.5
- shift: float32 [128], replicated, may hold values from -3 to 3
- cotangent: bfloat16 [16, 8, 1024, 128], P('bx', 'by'), may hold values from -13 to 13
Outputs:
- activated: bfloat16 [16, 8, 1024, 128], P('bx', 'by')
- grad_features: bfloat16 [16, 8, 1024, 128], P('bx', 'by')
- grad_weight: float32 [27, 128, 128], P(None, 'bx', 'by')
Inputs may be any that keep to these rules, and one draw needn't show every extreme that they name: Rows 0 to live_count - 1 of a brick are live, the rest padding; in every draw some brick is full. `send_rows`: every entry is below its brick's live count; the eight blocks follow the directions (dx, dy) in row-major order with the brick's own position left out. `neighbour_map`: entries index the brick's extended table; offset 13 of a live row names that row itself; every entry of a padding row is 1536. With B = min(1024, 512) and q = r // B for a live row r, an entry below 1024 lies in rows q B to q B + B - 1, and an entry 1024 + b * 128 + h of incoming block b other than 4 has h in q * 128 B / 1024 to (q + 1) * 128 B / 1024 - 1.
All inputs are finite; a program needn't handle non-finite values.
Results may differ from a plain program's by a relative error of at most 0.029.
The roundings to bfloat16 on the way count: a program that leaves them out, or rounds other values in their place, can miss the bound.
Values may be sent and summed in bfloat16 or wider, within the bound.
No kernel may reach another device: no remote copies, remote signals or barrier semaphores. Data moves between devices by JAX's collectives and lax.ppermute only.
A program may use at most 64 MiB of HBM per device.

v0:
```python
import jax
import jax.numpy as jnp
from jax import lax
from jax.sharding import PartitionSpec as P

epsilon = 1e-05


def extended(cells, sides, width):
    for axis, dim in sides:
        count = lax.axis_size(axis)
        ends = count - 1
        head = lax.slice_in_dim(cells, 0, width, axis=dim)
        tail = lax.slice_in_dim(cells, cells.shape[dim] - width, cells.shape[dim], axis=dim)
        cells = jnp.concatenate(
            [
                lax.ppermute(tail, axis, [(i, (i + 1) % count) for i in range(ends)]),
                cells,
                lax.ppermute(head, axis, [((i + 1) % count, i) for i in range(ends)]),
            ],
            axis=dim,
        )
    return cells


def from_neighbours(outgoing):
    padded = extended(outgoing, (("bx", 0), ("by", 1)), 1)
    return padded[::2, ::2]


def per_device(features, live_count, neighbour_map, send_rows, weight, gain, shift, cotangent):
    own_rows = features[0, 0]
    rows_total, channels = own_rows.shape
    halo_rows = send_rows.shape[3]
    block_rows = min(rows_total, 512)
    blocks_count = rows_total // block_rows
    halo_window = halo_rows // blocks_count
    window_rows = block_rows + 9 * halo_window
    sent_index = send_rows[0, 0].reshape(-1)
    send_select = (
        sent_index[:, None] == lax.broadcasted_iota(jnp.int32, (1, rows_total), 1)
    ).astype(jnp.bfloat16)
    chosen_rows = jnp.dot(send_select, own_rows, preferred_element_type=jnp.float32).astype(
        jnp.bfloat16
    )
    chosen_rows = chosen_rows.reshape(8, halo_rows, channels)
    blank_block = jnp.zeros((1, halo_rows, channels), jnp.bfloat16)
    outgoing = jnp.concatenate([chosen_rows[:4], blank_block, chosen_rows[4:]], axis=0).reshape(
        3, 3, halo_rows, channels
    )
    incoming = from_neighbours(outgoing).reshape(9, blocks_count, halo_window, channels)
    index_blocks = neighbour_map[0, 0].reshape(27, blocks_count, block_rows).transpose(1, 0, 2)
    own_blocks = own_rows.reshape(blocks_count, block_rows, channels)
    halo_blocks = incoming.transpose(1, 0, 2, 3)
    block_ids = jnp.arange(blocks_count, dtype=jnp.int32)

    def selector_of(indices, block_index):
        beyond = indices - rows_total
        target = beyond // halo_rows
        inside = beyond - target * halo_rows - block_index * halo_window
        local_pos = indices - block_index * block_rows
        remote_pos = block_rows + target * halo_window + inside
        usable = (inside >= 0) & (inside < halo_window)
        position = jnp.where(indices < rows_total, local_pos, jnp.where(usable, remote_pos, -1))
        return position[:, :, None] == lax.broadcasted_iota(jnp.int32, (1, 1, window_rows), 2)

    def forward_block(pieces):
        indices, own_part, halo_part, block_index = pieces
        window = jnp.concatenate([own_part, halo_part.reshape(9 * halo_window, channels)], axis=0)
        selector = selector_of(indices, block_index).astype(jnp.bfloat16)
        gathered = jnp.einsum(
            "kbw,wc->bkc", selector, window, preferred_element_type=jnp.float32
        ).astype(jnp.bfloat16)
        columns = gathered.reshape(block_rows, 27 * channels)
        return (jnp.dot(columns, weight, preferred_element_type=jnp.float32), columns)

    conv_blocks, column_blocks = lax.map(
        forward_block, (index_blocks, own_blocks, halo_blocks, block_ids)
    )
    conv_out = conv_blocks.reshape(rows_total, channels).astype(jnp.bfloat16)
    conv_float = conv_out.astype(jnp.float32)
    live_mask = (lax.broadcasted_iota(jnp.int32, (rows_total, 1), 0) < live_count[0, 0]).astype(
        jnp.float32
    )
    local_count = jnp.sum(live_mask)
    total_sum, total_count = lax.psum(
        (jnp.sum(conv_float * live_mask, axis=0), local_count), ("bx", "by")
    )
    center = total_sum / total_count
    deviation = (conv_float - center) * live_mask
    variance = lax.psum(jnp.sum(deviation * deviation, axis=0), ("bx", "by")) / total_count
    inverse_std = lax.rsqrt(variance + epsilon)
    normalized = (conv_float - center) * inverse_std
    before = gain * normalized + shift
    activated = (jnp.maximum(before, 0.0) * live_mask).astype(jnp.bfloat16)
    upstream = cotangent[0, 0].astype(jnp.float32) * (before > 0.0) * live_mask
    sum_up, sum_cross = lax.psum(
        (jnp.sum(upstream, axis=0), jnp.sum(upstream * normalized, axis=0)), ("bx", "by")
    )
    conv_grad = (
        gain
        * inverse_std
        * (upstream - live_mask * (sum_up + normalized * sum_cross) / total_count)
    ).astype(jnp.bfloat16)
    grad_blocks = conv_grad.reshape(blocks_count, block_rows, channels)

    def backward_block(weight_acc, pieces):
        indices, columns, grad_rows, block_index = pieces
        weight_acc = weight_acc + lax.dot_general(
            columns, grad_rows, (((0,), (0,)), ((), ())), preferred_element_type=jnp.float32
        )
        column_grad = lax.dot_general(
            grad_rows, weight, (((1,), (1,)), ((), ())), preferred_element_type=jnp.float32
        )
        column_grad = column_grad.reshape(block_rows, 27, channels)
        selector = selector_of(indices, block_index).astype(jnp.float32)
        window_grad = jnp.einsum(
            "kbw,bkc->wc",
            selector,
            column_grad,
            precision=lax.Precision.HIGHEST,
            preferred_element_type=jnp.float32,
        )
        return (
            weight_acc,
            (window_grad[:block_rows], window_grad[block_rows:].reshape(9, halo_window, channels)),
        )

    start_acc = jnp.zeros((27 * channels, channels), jnp.float32)
    weight_acc, (own_parts, halo_parts) = lax.scan(
        backward_block, start_acc, (index_blocks, column_blocks, grad_blocks, block_ids)
    )
    weight_terms = weight_acc.reshape(27, channels, channels)
    partial_x = lax.psum_scatter(
        weight_terms.astype(jnp.bfloat16), "bx", scatter_dimension=1, tiled=True
    )
    summed = lax.psum_scatter(partial_x, "by", scatter_dimension=2, tiled=True).astype(jnp.float32)
    grad_weight = summed / jnp.sqrt(total_count)
    own_table = own_parts.reshape(rows_total, channels)
    halo_table = halo_parts.transpose(1, 0, 2, 3).reshape(3, 3, halo_rows, channels)
    halo_grad = halo_table.astype(jnp.bfloat16)
    returned = from_neighbours(halo_grad).reshape(9, halo_rows, channels)
    slots_back = (
        jnp.concatenate([returned[:4], returned[5:]], axis=0)
        .reshape(-1, channels)
        .astype(jnp.float32)
    )
    added_back = lax.dot_general(
        send_select.astype(jnp.float32),
        slots_back,
        (((0,), (0,)), ((), ())),
        precision=lax.Precision.HIGHEST,
        preferred_element_type=jnp.float32,
    )
    own_grad = own_table + added_back
    return (activated[None, None], own_grad.astype(jnp.bfloat16)[None, None], grad_weight)


def solution(mesh):
    return jax.shard_map(
        per_device,
        mesh=mesh,
        in_specs=(
            P("bx", "by", None, None),
            P("bx", "by"),
            P("bx", "by", None, None),
            P("bx", "by", None, None),
            P(),
            P(),
            P(),
            P("bx", "by", None, None),
        ),
        out_specs=(P("bx", "by", None, None), P("bx", "by", None, None), P(None, "bx", "by")),
        check_vma=False,
    )
```

profile of v0, /device:TPU:0, one launch (start us, length us, event | category | flops | bytes accessed | tf_op | source)
XLA Modules:
  0.0 465.1 jit_solution(409183118276341036)
XLA Ops:
  7.2 1.9 fusion.34
  9.1 3.9 collective-permute-start
  13.0 1.3 collective-permute-start.1
  15.2 4.3 collective-permute-done.1
  19.5 0.8 pad_maximum_fusion.9
  20.3 1.9 collective-permute-start.2
  22.2 1.3 collective-permute-start.3
  23.6 1.2 reduce.4
  25.5 1.5 collective-permute-done.3
  27.0 1.1 pad_maximum_fusion
  28.2 38.2 %while.33 = (s32[]{:T(128)}, bf16[2,512,128]{2,1,0:T(8,128)(2,1)S(1)}, bf16[2,512,3456]{1,2,0:T(8,128)(2,1)}, bf16[2,512,128]{2,1,0:T(8,128)(2,1)}, bf16[2,9,64,...) while((s32[]{:T(128)}, ...), condition=%wide.region_1.2_spmd.clone, body=%wide.region_0.1_spmd.sunk.clone | while | flops 4321123840 | bytes 16304801 | solution.py:77
  30.2 0.9 dynamic-slice_bitcast_fusion.3
  31.2 13.0 %fusion.82 = bf16[128,27,512]{2,0,1:T(8,128)(2,1)S(1)} fusion(s32[27,512]{1,0:T(8,128)S(1)} %bitcast_select_fusion.6, bf16[576,128]{1,0:T(8,128)(2,1)S(1)} %bitcast.223, bf16[512,128]{1,0:T(8,128)(2,1)S(1)} %dynamic-slice_bitcast_fusion.3), kind=kOutput, calls=%fused_computation.3.clone.1.clone | convolution fusion | flops 3867738112 | bytes 3872768 | tf_op jit(solution)/shard_map/while/body/eval_jaxpr/kbw,wc->bkc/dot_general | solution.py:71
  44.1 2.0 constant_dynamic-update-slice_fusion.6
  46.1 1.2 fusion.83
  49.3 0.9 dynamic-slice_bitcast_fusion.3
  50.2 13.0 %fusion.82 = bf16[128,27,512]{2,0,1:T(8,128)(2,1)S(1)} fusion(s32[27,512]{1,0:T(8,128)S(1)} %bitcast_select_fusion.6, bf16[576,128]{1,0:T(8,128)(2,1)S(1)} %bitcast.223, bf16[512,128]{1,0:T(8,128)(2,1)S(1)} %dynamic-slice_bitcast_fusion.3), kind=kOutput, calls=%fused_computation.3.clone.1.clone | convolution fusion | flops 3867738112 | bytes 3872768 | tf_op jit(solution)/shard_map/while/body/eval_jaxpr/kbw,wc->bkc/dot_general | solution.py:71
  63.2 2.0 constant_dynamic-update-slice_fusion.6
  65.2 1.2 fusion.83
  66.6 70.3 %all-reduce.2 = (f32[128]{0:T(128)S(1)}, f32[]{:T(128)}) all-reduce(f32[128]{0:T(128)S(1)} %multiply_reduce_fusion.1, f32[]{:T(128)} %fusion.44), channel_id=1, replica_groups=mesh['bx'=16,'by'=8] {'bx','by'}, use_global_device_ids=true, to_apply=%region_3.4 | all-reduce | flops 129 | bytes 1032 | tf_op jit(solution)/shard_map/psum | solution.py:86
  137.8 62.7 %psum.37 = f32[128]{0:T(128)S(1)} all-reduce(f32[128]{0:T(128)S(1)} %multiply_reduce_fusion), channel_id=1, replica_groups=mesh['bx'=16,'by'=8] {'bx','by'}, use_global_device_ids=true, to_apply=%region_7.8 | all-reduce | flops 128 | bytes 1024 | tf_op jit(solution)/shard_map/psum | solution.py:91
  201.2 1.2 fusion.39
  202.4 64.2 %all-reduce.1 = (f32[128]{0:T(128)S(1)}, f32[128]{0:T(128)S(1)}) all-reduce(f32[128]{0:T(128)S(1)} %get-tuple-element.329, f32[128]{0:T(128)S(1)} %get-tuple-element.328), channel_id=1, replica_groups=mesh['bx'=16,'by'=8] {'bx','by'}, use_global_device_ids=true, to_apply=%region_11.12 | all-reduce | flops 256 | bytes 2048 | tf_op jit(solution)/shard_map/psum | solution.py:97
  266.6 1.9 fusion.42
  268.5 73.1 %while.34 = (s32[]{:T(128)}, f32[3456,128]{1,0:T(8,128)S(1)}, f32[2,512,128]{2,1,0:T(8,128)}, bf16[2,9,64,128]{3,2,0,1:T(8,128)(2,1)}, bf16[2,512,3456]{1,2,0:T(...) while((s32[]{:T(128)}, f32[3456,128]{1,0:T(8,128)S(1)}, ...), condition=%wide.region_13.14_spmd.clone.clone, body=%wide.region_12.13_spmd.clone.sunk.clone | while | flops 24024522752 | bytes 28413672 | solution.py:130
  270.5 1.1 fusion.89
  271.6 28.7 %fusion.90 = f32[1088,128]{1,0:T(8,128)S(1)} fusion(f32[512,27,128]{2,0,1:T(8,128)S(1)} %fusion.89, s32[27,512]{1,0:T(8,128)S(1)} %bitcast_select_fusion.7), kind=kOutput, calls=%fused_computation.31.clone.1.clone | convolution fusion | flops 23117266944 | bytes 7690240 | tf_op jit(solution)/shard_map/while/body/eval_jaxpr/kbw,bkc->wc/dot_general | solution.py:117
  301.8 3.2 convolution_add_fusion.3
  307.1 1.1 fusion.89
  308.2 28.7 %fusion.90 = f32[1088,128]{1,0:T(8,128)S(1)} fusion(f32[512,27,128]{2,0,1:T(8,128)S(1)} %fusion.89, s32[27,512]{1,0:T(8,128)S(1)} %bitcast_select_fusion.7), kind=kOutput, calls=%fused_computation.31.clone.1.clone | convolution fusion | flops 23117266944 | bytes 7690240 | tf_op jit(solution)/shard_map/while/body/eval_jaxpr/kbw,bkc->wc/dot_general | solution.py:117
  338.4 3.2 convolution_add_fusion.3
  341.7 1.0 convert_element_type.131
  342.8 1.0 fusion.48
  343.7 1.3 collective-permute-start.4
  345.0 1.3 collective-permute-start.5
  348.3 4.0 collective-permute-done.5
  352.3 1.0 pad_maximum_fusion.6
  353.3 1.5 collective-permute-start.6
  354.8 1.3 collective-permute-start.7
  356.1 0.9 multiply_convert_fusion
  357.1 2.2 collective-permute-done.7
  359.3 1.1 pad_maximum_fusion.1
  360.5 64.4 %all-reduce.5.cloned.1.call-done = bf16[27,128,128]{2,1,0:T(8,128)(2,1)} async-done(((bf16[27,128,128]{2,1,0:T(8,128)(2,1)}), bf16[27,128,128]{2,1,0:T(8,128)(2,1)}) %all-reduce.5.cloned.1.call-update) | async-done | bytes 884752
  424.9 0.8 constant_dynamic-slice_fusion.1
  425.7 0.9 copy.30
  426.7 3.2 fusion.35
  429.9 27.0 %reduce-scatter.3.cloned.1.call-done = bf16[27,8,16]{0,1,2:T(8,128)(2,1)} async-done(((bf16[27,8,128]{0,1,2:T(8,128)(2,1)}), bf16[27,8,16]{0,1,2:T(8,128)(2,1)}) %reduce-scatter.3.cloned.1.call-update) | async-done | bytes 6928 | tf_op jit(solution)/shard_map/reduce_scatter | solution.py:137
  456.9 0.8 convert_divide_fusion
  (68 shorter events, 9.9 us)
Async XLA Ops:
  7.2 21.0 %copy-start = (bf16[3456,128]{1,0:T(8,128)(2,1)S(1)}, bf16[3456,128]{1,0:T(8,128)(2,1)}, u32[]{:S(2)}) copy-start(bf16[3456,128]{1,0:T(8,128)(2,1)} %param.16) | copy-start | bytes 2654212
  7.2 417.8 %all-reduce.5.cloned.1.call-start = ((), (), s32[]{:S(2)}) async-start(), calls=%async_computation.2 | async-start | bytes 1769472
  9.1 6.1 %collective-permute-start = (bf16[1,3,128,128]{3,2,1,0:T(8,128)(2,1)S(1)}, bf16[1,3,128,128]{3,2,1,0:T(8,128)(2,1)S(1)}, u32[]{:S(2)}, u32[]{:S(2)}) collective-permute-start(bf16[1,3,128,128]{3,2,1,0:T(8,128)(2,1)S(1)} %bitcast.239), channel_id=1, source_target_pairs={{0,8},{8,16},{16,24},{24,32},{32,40},{40,48},{48,56},{56,64},{64,7... | collective-permute-start | bytes 294920 | tf_op jit(solution)/shard_map/ppermute | solution.py:17
  13.0 6.5 %collective-permute-start.1 = (bf16[1,3,128,128]{3,2,1,0:T(8,128)(2,1)S(1)}, bf16[1,3,128,128]{3,2,1,0:T(8,128)(2,1)S(1)}, u32[]{:S(2)}, u32[]{:S(2)}) collective-permute-start(bf16[1,3,128,128]{3,2,1,0:T(8,128)(2,1)S(1)} %bitcast.238), channel_id=1, source_target_pairs={{8,0},{16,8},{24,16},{32,24},{40,32},{48,40},{56,48},{64,56},{72,6... | collective-permute-start | bytes 294920 | tf_op jit(solution)/shard_map/ppermute | solution.py:19
  20.3 5.2 %collective-permute-start.2 = (bf16[5,1,128,128]{3,2,1,0:T(8,128)(2,1)}, bf16[5,1,128,128]{3,2,1,0:T(8,128)(2,1)}, u32[]{:S(2)}, u32[]{:S(2)}) collective-permute-start(bf16[5,1,128,128]{3,2,1,0:T(8,128)(2,1)} %get-tuple-element.372), channel_id=1, source_target_pairs={{0,1},{1,2},{2,3},{3,4},{4,5},{5,6},{6,7},{8,9},{9,10},{10,11},{11... | collective-permute-start | bytes 491528 | tf_op jit(solution)/shard_map/ppermute | solution.py:17
  22.2 4.8 %collective-permute-start.3 = (bf16[5,1,128,128]{3,2,1,0:T(8,128)(2,1)}, bf16[5,1,128,128]{3,2,1,0:T(8,128)(2,1)}, u32[]{:S(2)}, u32[]{:S(2)}) collective-permute-start(bf16[5,1,128,128]{3,2,1,0:T(8,128)(2,1)} %get-tuple-element.373), channel_id=1, source_target_pairs={{1,0},{2,1},{3,2},{4,3},{5,4},{6,5},{7,6},{9,8},{10,9},{11,10},{12... | collective-permute-start | bytes 491528 | tf_op jit(solution)/shard_map/ppermute | solution.py:19
  28.2 172.3 %copy-start.1 = (f32[128]{0:T(128)S(1)}, f32[128]{0:T(128)}, u32[]{:S(2)}) copy-start(f32[128]{0:T(128)} %param.17) | copy-start | bytes 1540
  28.2 173.0 %copy-start.2 = (f32[128]{0:T(128)S(1)}, f32[128]{0:T(128)}, u32[]{:S(2)}) copy-start(f32[128]{0:T(128)} %param.18) | copy-start | bytes 1540
  268.5 77.9 %copy-start.6 = (u32[128]{0:T(128)S(1)}, u32[128]{0:T(128)}, u32[]{:S(2)}) copy-start(u32[128]{0:T(128)} %constant.182) | copy-start | bytes 1540
  271.6 28.7 %copy-start.3 = (f32[2,512,128]{2,1,0:T(8,128)S(1)}, f32[2,512,128]{2,1,0:T(8,128)}, u32[]{:S(2)}) copy-start(f32[2,512,128]{2,1,0:T(8,128)} %get-tuple-element.580) | copy-start | bytes 1572868 | tf_op jit(solution)/shard_map/while
  300.4 0.8 copy-start.4
  308.1 28.7 %copy-start.3 = (f32[2,512,128]{2,1,0:T(8,128)S(1)}, f32[2,512,128]{2,1,0:T(8,128)}, u32[]{:S(2)}) copy-start(f32[2,512,128]{2,1,0:T(8,128)} %get-tuple-element.580) | copy-start | bytes 1572868 | tf_op jit(solution)/shard_map/while
  336.9 0.8 copy-start.4
  341.6 85.0 %copy-start.5 = (s32[1,1,8,128]{3,2,1,0:T(8,128)S(1)}, s32[1,1,8,128]{3,2,1,0:T(8,128)}, u32[]{:S(2)}) copy-start(s32[1,1,8,128]{3,2,1,0:T(8,128)} %param.15) | copy-start | bytes 12292
  342.7 114.2 %reduce-scatter.3.cloned.1.call-start = ((), (), s32[]{:S(2)}) async-start(), calls=%async_computation.1 | async-start | bytes 294912 | tf_op jit(solution)/shard_map/reduce_scatter | solution.py:137
  343.7 4.6 collective-permute-start.4
  345.0 7.3 %collective-permute-start.5 = (bf16[1,3,128,128]{3,2,1,0:T(8,128)(2,1)S(1)}, bf16[1,3,128,128]{3,2,1,0:T(8,128)(2,1)S(1)}, u32[]{:S(2)}, u32[]{:S(2)}) collective-permute-start(bf16[1,3,128,128]{3,2,1,0:T(8,128)(2,1)S(1)} %bitcast.236), channel_id=1, source_target_pairs={{8,0},{16,8},{24,16},{32,24},{40,32},{48,40},{56,48},{64,56},{72,6... | collective-permute-start | bytes 294920 | tf_op jit(solution)/shard_map/ppermute | solution.py:19
  353.3 3.7 collective-permute-start.6
  354.8 4.5 collective-permute-start.7
Sparse Core Ops, SparseCore 0:
  342.8 82.0 all-reduce.4
  427.3 29.5 reduce-scatter.2
where the time goes:
time: 466 us; the launch traced here: 465 us
  blocking collectives  197 us (42%)
  waiting for transfers between devices  104 us (22%)
  matrix products  99.4 us (21%)
  between operations  16.4 us (4%)
  local copies, waits for them, and re-layouts  15.4 us (3%)
  starting transfers between devices  13.9 us (3%)
  other arithmetic  13.7 us (3%)
  loops' own time  5.44 us (1%)
    psum x1, blocking collectives, per_device(): lax.psum((jnp.sum(conv_float * live_mask, axis=0), local_count), ('bx', '...  70.3 us
    unnamed x3, waiting for transfers between devices  64.5 us
    psum x1, blocking collectives, per_device(): lax.psum((jnp.sum(upstream, axis=0), jnp.sum(upstream * normalized, axis=...  64.2 us
    psum x1, blocking collectives, per_device(): lax.psum(jnp.sum(deviation * deviation, axis=0), ('bx', 'by')) / total_count  62.7 us
    dot_general x2, matrix products, backward_block(): jnp.einsum('kbw,bkc->wc', selector, column_grad, precision=lax.Precision....  57.4 us
    reduce_scatter x1, waiting for transfers between devices, per_device(): lax.psum_scatter(partial_x, 'by', scatter_dimension=2, tiled=True)  27 us
    dot_general x2, matrix products, forward_block(): jnp.einsum('kbw,wc->bkc', selector, window, preferred_element_type=jnp.fl...  25.9 us
    ppermute x4, waiting for transfers between devices, extended(): lax.ppermute(head, axis, [((i + 1) % count, i) for i in range(ends)])  12.1 us
  transfers between devices with their start and end apart: 10, of which 6 were waited for; matrix products, arithmetic and copies ran while one was open for 2% of the time, Pallas kernels for 0%

commit v1 on v0

--- a/solution.py
+++ b/solution.py
@@ -95,7 +95,7 @@
     activated = (jnp.maximum(before, 0.0) * live_mask).astype(jnp.bfloat16)
     upstream = cotangent[0, 0].astype(jnp.float32) * (before > 0.0) * live_mask
     sum_up, sum_cross = lax.psum(
-        (jnp.sum(upstream, axis=0), jnp.sum(upstream * normalized, axis=0)), ("bx", "by")
+        lax.psum((jnp.sum(upstream, axis=0), jnp.sum(upstream * normalized, axis=0)), "by"), "bx"
     )
     conv_grad = (
         gain

time: 466 us -> 451 us (0.968)
  blocking collectives: 197 us -> 184 us
    psum x1, blocking collectives: 64.2 us -> 13.9 us  [per_device(): lax.psum((jnp.sum(upstream, axis=0), jnp.sum(upstream * normalized, axis=...]
    psum x0 -> x1, blocking collectives: none -> 37.1 us  [per_device(): lax.psum(lax.psum((jnp.sum(upstream, axis=0), jnp.sum(upstream * normaliz...]
where the time goes in v1:
time: 451 us; the launch traced here: 450 us
  blocking collectives  184 us (41%)
  waiting for transfers between devices  100 us (22%)
  matrix products  99.4 us (22%)
  between operations  16.4 us (4%)
  local copies, waits for them, and re-layouts  15.5 us (3%)
  starting transfers between devices  14.9 us (3%)
  other arithmetic  13.7 us (3%)
  loops' own time  5.44 us (1%)
    psum x1, blocking collectives, per_device(): lax.psum((jnp.sum(conv_float * live_mask, axis=0), local_count), ('bx', '...  70.3 us
    psum x1, blocking collectives, per_device(): lax.psum(jnp.sum(deviation * deviation, axis=0), ('bx', 'by')) / total_count  62.7 us
    unnamed x3, waiting for transfers between devices  62.5 us
    dot_general x2, matrix products, backward_block(): jnp.einsum('kbw,bkc->wc', selector, column_grad, precision=lax.Precision....  57.4 us
    psum x1, blocking collectives, per_device(): lax.psum(lax.psum((jnp.sum(upstream, axis=0), jnp.sum(upstream * normaliz...  37.1 us
    reduce_scatter x1, waiting for transfers between devices, per_device(): lax.psum_scatter(partial_x, 'by', scatter_dimension=2, tiled=True)  27 us
    dot_general x2, matrix products, forward_block(): jnp.einsum('kbw,wc->bkc', selector, window, preferred_element_type=jnp.fl...  25.9 us
    psum x1, blocking collectives, per_device(): lax.psum((jnp.sum(upstream, axis=0), jnp.sum(upstream * normalized, axis=...  13.9 us
  transfers between devices with their start and end apart: 10, of which 6 were waited for; matrix products, arithmetic and copies ran while one was open for 2% of the time, Pallas kernels for 0%

profile of v1, /device:TPU:0, one launch (start us, length us, event | category | flops | bytes accessed | tf_op | source)
XLA Modules:
  0.0 449.6 jit_solution(4440683853368022679)
XLA Ops:
  7.2 1.9 fusion.34
  9.1 3.9 collective-permute-start
  13.0 1.3 collective-permute-start.1
  15.2 4.3 collective-permute-done.1
  20.3 1.9 collective-permute-start.2
  22.2 1.3 collective-permute-start.3
  23.6 1.2 reduce.4
  25.5 1.5 collective-permute-done.3
  27.0 1.1 pad_maximum_fusion
  28.2 38.2 %while.33 = (s32[]{:T(128)}, bf16[2,512,128]{2,1,0:T(8,128)(2,1)S(1)}, bf16[2,512,3456]{1,2,0:T(8,128)(2,1)}, bf16[2,512,128]{2,1,0:T(8,128)(2,1)}, bf16[2,9,64,...) while((s32[]{:T(128)}, ...), condition=%wide.region_1.2_spmd.clone, body=%wide.region_0.1_spmd.sunk.clone | while | flops 4321123840 | bytes 16304801 | solution.py:77
  30.2 0.9 dynamic-slice_bitcast_fusion.3
  31.2 13.0 %fusion.82 = bf16[128,27,512]{2,0,1:T(8,128)(2,1)S(1)} fusion(s32[27,512]{1,0:T(8,128)S(1)} %bitcast_select_fusion.6, bf16[576,128]{1,0:T(8,128)(2,1)S(1)} %bitcast.223, bf16[512,128]{1,0:T(8,128)(2,1)S(1)} %dynamic-slice_bitcast_fusion.3), kind=kOutput, calls=%fused_computation.3.clone.1.clone | convolution fusion | flops 3867738112 | bytes 3872768 | tf_op jit(solution)/shard_map/while/body/eval_jaxpr/kbw,wc->bkc/dot_general | solution.py:71
  44.1 2.0 constant_dynamic-update-slice_fusion.6
  46.1 1.2 fusion.83
  49.3 0.9 dynamic-slice_bitcast_fusion.3
  50.2 13.0 %fusion.82 = bf16[128,27,512]{2,0,1:T(8,128)(2,1)S(1)} fusion(s32[27,512]{1,0:T(8,128)S(1)} %bitcast_select_fusion.6, bf16[576,128]{1,0:T(8,128)(2,1)S(1)} %bitcast.223, bf16[512,128]{1,0:T(8,128)(2,1)S(1)} %dynamic-slice_bitcast_fusion.3), kind=kOutput, calls=%fused_computation.3.clone.1.clone | convolution fusion | flops 3867738112 | bytes 3872768 | tf_op jit(solution)/shard_map/while/body/eval_jaxpr/kbw,wc->bkc/dot_general | solution.py:71
  63.2 2.0 constant_dynamic-update-slice_fusion.6
  65.3 1.2 fusion.83
  66.7 70.3 %all-reduce.1 = (f32[128]{0:T(128)S(1)}, f32[]{:T(128)}) all-reduce(f32[128]{0:T(128)S(1)} %multiply_reduce_fusion.1, f32[]{:T(128)} %fusion.44), channel_id=1, replica_groups=mesh['bx'=16,'by'=8] {'bx','by'}, use_global_device_ids=true, to_apply=%region_3.4 | all-reduce | flops 129 | bytes 1032 | tf_op jit(solution)/shard_map/psum | solution.py:86
  137.8 62.7 %psum.51 = f32[128]{0:T(128)S(1)} all-reduce(f32[128]{0:T(128)S(1)} %multiply_reduce_fusion), channel_id=1, replica_groups=mesh['bx'=16,'by'=8] {'bx','by'}, use_global_device_ids=true, to_apply=%region_7.8 | all-reduce | flops 128 | bytes 1024 | tf_op jit(solution)/shard_map/psum | solution.py:91
  201.2 1.2 fusion.39
  202.4 13.9 %all-reduce.3 = (f32[128]{0:T(128)S(1)}, f32[128]{0:T(128)S(1)}) all-reduce(f32[128]{0:T(128)S(1)} %get-tuple-element.329, f32[128]{0:T(128)S(1)} %get-tuple-element.328), channel_id=1, replica_groups=mesh['bx'=16,'by'=8] {'by'}, use_global_device_ids=true, to_apply=%region_12.13 | all-reduce | flops 256 | bytes 2048 | tf_op jit(solution)/shard_map/psum | solution.py:98
  216.2 37.1 %all-reduce.2 = (f32[128]{0:T(128)S(1)}, f32[128]{0:T(128)S(1)}) all-reduce(f32[128]{0:T(128)S(1)} %get-tuple-element.368, f32[128]{0:T(128)S(1)} %get-tuple-element.369), channel_id=1, replica_groups=mesh['bx'=16,'by'=8] {'bx'}, use_global_device_ids=true, to_apply=%region_13.14 | all-reduce | flops 256 | bytes 2048 | tf_op jit(solution)/shard_map/psum | solution.py:97
  253.3 1.9 fusion.42
  255.2 73.2 %while.34 = (s32[]{:T(128)}, f32[3456,128]{1,0:T(8,128)S(1)}, f32[2,512,128]{2,1,0:T(8,128)}, bf16[2,9,64,128]{3,2,0,1:T(8,128)(2,1)}, bf16[2,512,3456]{1,2,0:T(...) while((s32[]{:T(128)}, f32[3456,128]{1,0:T(8,128)S(1)}, ...), condition=%wide.region_15.16_spmd.clone.clone, body=%wide.region_14.15_spmd.clone.sunk.clone | while | flops 24024522752 | bytes 28413672 | solution.py:130
  257.2 1.1 fusion.89
  258.3 28.7 %fusion.90 = f32[1088,128]{1,0:T(8,128)S(1)} fusion(f32[512,27,128]{2,0,1:T(8,128)S(1)} %fusion.89, s32[27,512]{1,0:T(8,128)S(1)} %bitcast_select_fusion.7), kind=kOutput, calls=%fused_computation.31.clone.1.clone | convolution fusion | flops 23117266944 | bytes 7690240 | tf_op jit(solution)/shard_map/while/body/eval_jaxpr/kbw,bkc->wc/dot_general | solution.py:117
  288.6 3.2 convolution_add_fusion.3
  293.8 1.1 fusion.89
  294.9 28.7 %fusion.90 = f32[1088,128]{1,0:T(8,128)S(1)} fusion(f32[512,27,128]{2,0,1:T(8,128)S(1)} %fusion.89, s32[27,512]{1,0:T(8,128)S(1)} %bitcast_select_fusion.7), kind=kOutput, calls=%fused_computation.31.clone.1.clone | convolution fusion | flops 23117266944 | bytes 7690240 | tf_op jit(solution)/shard_map/while/body/eval_jaxpr/kbw,bkc->wc/dot_general | solution.py:117
  325.1 3.2 convolution_add_fusion.3
  328.4 1.0 convert_element_type.131
  329.5 1.0 fusion.48
  330.5 2.5 collective-permute-start.4
  333.0 1.3 collective-permute-start.5
  336.2 4.0 collective-permute-done.5
  340.2 1.0 pad_maximum_fusion.6
  341.2 1.3 collective-permute-start.6
  342.5 1.3 collective-permute-start.7
  343.8 0.9 multiply_convert_fusion
  344.7 1.1 collective-permute-done.7
  345.8 1.1 pad_maximum_fusion.1
  346.9 62.5 %all-reduce.6.cloned.1.call-done = bf16[27,128,128]{2,1,0:T(8,128)(2,1)} async-done(((bf16[27,128,128]{2,1,0:T(8,128)(2,1)}), bf16[27,128,128]{2,1,0:T(8,128)(2,1)}) %all-reduce.6.cloned.1.call-update) | async-done | bytes 884752
  409.4 0.8 constant_dynamic-slice_fusion.1
  410.2 0.9 copy.30
  411.2 3.2 fusion.35
  414.4 27.0 %reduce-scatter.3.cloned.1.call-done = bf16[27,8,16]{0,1,2:T(8,128)(2,1)} async-done(((bf16[27,8,128]{0,1,2:T(8,128)(2,1)}), bf16[27,8,16]{0,1,2:T(8,128)(2,1)}) %reduce-scatter.3.cloned.1.call-update) | async-done | bytes 6928 | tf_op jit(solution)/shard_map/reduce_scatter | solution.py:137
  441.4 0.8 convert_divide_fusion
  (69 shorter events, 10.6 us)
Async XLA Ops:
  7.2 21.0 %copy-start = (bf16[3456,128]{1,0:T(8,128)(2,1)S(1)}, bf16[3456,128]{1,0:T(8,128)(2,1)}, u32[]{:S(2)}) copy-start(bf16[3456,128]{1,0:T(8,128)(2,1)} %param.16) | copy-start | bytes 2654212
  7.2 402.3 %all-reduce.6.cloned.1.call-start = ((), (), s32[]{:S(2)}) async-start(), calls=%async_computation.2 | async-start | bytes 1769472
  9.1 6.1 %collective-permute-start = (bf16[1,3,128,128]{3,2,1,0:T(8,128)(2,1)S(1)}, bf16[1,3,128,128]{3,2,1,0:T(8,128)(2,1)S(1)}, u32[]{:S(2)}, u32[]{:S(2)}) collective-permute-start(bf16[1,3,128,128]{3,2,1,0:T(8,128)(2,1)S(1)} %bitcast.239), channel_id=1, source_target_pairs={{0,8},{8,16},{16,24},{24,32},{32,40},{40,48},{48,56},{56,64},{64,7... | collective-permute-start | bytes 294920 | tf_op jit(solution)/shard_map/ppermute | solution.py:17
  13.0 6.5 %collective-permute-start.1 = (bf16[1,3,128,128]{3,2,1,0:T(8,128)(2,1)S(1)}, bf16[1,3,128,128]{3,2,1,0:T(8,128)(2,1)S(1)}, u32[]{:S(2)}, u32[]{:S(2)}) collective-permute-start(bf16[1,3,128,128]{3,2,1,0:T(8,128)(2,1)S(1)} %bitcast.238), channel_id=1, source_target_pairs={{8,0},{16,8},{24,16},{32,24},{40,32},{48,40},{56,48},{64,56},{72,6... | collective-permute-start | bytes 294920 | tf_op jit(solution)/shard_map/ppermute | solution.py:19
  20.3 5.2 %collective-permute-start.2 = (bf16[5,1,128,128]{3,2,1,0:T(8,128)(2,1)}, bf16[5,1,128,128]{3,2,1,0:T(8,128)(2,1)}, u32[]{:S(2)}, u32[]{:S(2)}) collective-permute-start(bf16[5,1,128,128]{3,2,1,0:T(8,128)(2,1)} %get-tuple-element.374), channel_id=1, source_target_pairs={{0,1},{1,2},{2,3},{3,4},{4,5},{5,6},{6,7},{8,9},{9,10},{10,11},{11... | collective-permute-start | bytes 491528 | tf_op jit(solution)/shard_map/ppermute | solution.py:17
  22.2 4.8 %collective-permute-start.3 = (bf16[5,1,128,128]{3,2,1,0:T(8,128)(2,1)}, bf16[5,1,128,128]{3,2,1,0:T(8,128)(2,1)}, u32[]{:S(2)}, u32[]{:S(2)}) collective-permute-start(bf16[5,1,128,128]{3,2,1,0:T(8,128)(2,1)} %get-tuple-element.375), channel_id=1, source_target_pairs={{1,0},{2,1},{3,2},{4,3},{5,4},{6,5},{7,6},{9,8},{10,9},{11,10},{12... | collective-permute-start | bytes 491528 | tf_op jit(solution)/shard_map/ppermute | solution.py:19
  28.2 172.3 %copy-start.1 = (f32[128]{0:T(128)S(1)}, f32[128]{0:T(128)}, u32[]{:S(2)}) copy-start(f32[128]{0:T(128)} %param.17) | copy-start | bytes 1540
  28.2 173.0 %copy-start.2 = (f32[128]{0:T(128)S(1)}, f32[128]{0:T(128)}, u32[]{:S(2)}) copy-start(f32[128]{0:T(128)} %param.18) | copy-start | bytes 1540
  255.2 79.0 %copy-start.6 = (u32[128]{0:T(128)S(1)}, u32[128]{0:T(128)}, u32[]{:S(2)}) copy-start(u32[128]{0:T(128)} %constant.182) | copy-start | bytes 1540
  258.3 28.7 %copy-start.3 = (f32[2,512,128]{2,1,0:T(8,128)S(1)}, f32[2,512,128]{2,1,0:T(8,128)}, u32[]{:S(2)}) copy-start(f32[2,512,128]{2,1,0:T(8,128)} %get-tuple-element.582) | copy-start | bytes 1572868 | tf_op jit(solution)/shard_map/while
  287.1 0.8 copy-start.4
  294.9 28.7 %copy-start.3 = (f32[2,512,128]{2,1,0:T(8,128)S(1)}, f32[2,512,128]{2,1,0:T(8,128)}, u32[]{:S(2)}) copy-start(f32[2,512,128]{2,1,0:T(8,128)} %get-tuple-element.582) | copy-start | bytes 1572868 | tf_op jit(solution)/shard_map/while
  323.7 0.8 copy-start.4
  328.4 82.8 %copy-start.5 = (s32[1,1,8,128]{3,2,1,0:T(8,128)S(1)}, s32[1,1,8,128]{3,2,1,0:T(8,128)}, u32[]{:S(2)}) copy-start(s32[1,1,8,128]{3,2,1,0:T(8,128)} %param.15) | copy-start | bytes 12292
  329.5 111.9 %reduce-scatter.3.cloned.1.call-start = ((), (), s32[]{:S(2)}) async-start(), calls=%async_computation.1 | async-start | bytes 294912 | tf_op jit(solution)/shard_map/reduce_scatter | solution.py:137
  330.5 5.7 %collective-permute-start.4 = (bf16[1,3,128,128]{3,2,1,0:T(8,128)(2,1)S(1)}, bf16[1,3,128,128]{3,2,1,0:T(8,128)(2,1)S(1)}, u32[]{:S(2)}, u32[]{:S(2)}) collective-permute-start(bf16[1,3,128,128]{3,2,1,0:T(8,128)(2,1)S(1)} %bitcast.237), channel_id=1, source_target_pairs={{0,8},{8,16},{16,24},{24,32},{32,40},{40,48},{48,56},{56,64},{64,7... | collective-permute-start | bytes 294920 | tf_op jit(solution)/shard_map/ppermute | solution.py:17
  333.0 7.2 %collective-permute-start.5 = (bf16[1,3,128,128]{3,2,1,0:T(8,128)(2,1)S(1)}, bf16[1,3,128,128]{3,2,1,0:T(8,128)(2,1)S(1)}, u32[]{:S(2)}, u32[]{:S(2)}) collective-permute-start(bf16[1,3,128,128]{3,2,1,0:T(8,128)(2,1)S(1)} %bitcast.236), channel_id=1, source_target_pairs={{8,0},{16,8},{24,16},{32,24},{40,32},{48,40},{56,48},{64,56},{72,6... | collective-permute-start | bytes 294920 | tf_op jit(solution)/shard_map/ppermute | solution.py:19
  341.2 3.5 collective-permute-start.6
  342.5 3.3 collective-permute-start.7
Sparse Core Ops, SparseCore 0:
  329.6 79.7 all-reduce.5
  411.8 29.5 reduce-scatter.2
